TPU v7x, 128 devices: a whole 4x4x4 slice. The times are simulated.
128 devices in a mesh: row: 16 (over z_hi, x, core), col: 8 (over y, z_lo).
Axes of the slice: x: 4, y: 4, z: 4 (z_hi: 2, z_lo: 2; z = z_hi * 2 + z_lo), core: 2. Of those that a mesh axis runs over, the one named last changes fastest.
Arguments:
- before_scan: float32 [4, 4096, 8192], P(None, 'row', 'col'), may hold values from -40 to 40
- after_scan: float32 [4, 4096, 8192], P(None, 'row', 'col'), may hold values from -40 to 40
- drift_offsets: int32 [2, 4, 16, 8], P(None, None, 'row', 'col'), may hold values from -128 to 128, as said below
- drift_fractions: int32 [2, 4, 16, 8], P(None, None, 'row', 'col'), may hold values from 0 to 255
Outputs:
- band_field: float32 [4, 4096, 8192], P(None, 'row', 'col')
- slope_field: float32 [4, 4096, 8192], P(None, 'row', 'col')
- surface_params: float32 [2, 4], replicated
Inputs may be any that keep to these rules, and one draw needn't show every extreme that they name: `drift_offsets`: for every scan and tile, the cells a tile reads (its own cells shifted by its offsets, widened by one row and column before and two after) lie inside the window. In every scan the first tile has offsets 128, 128 and the last tile minus 128, minus 128.
All inputs are finite; a program needn't handle non-finite values.
Results may differ from a plain program's by a relative error of at most 0.00014.
Values sent between devices are 32-bit elements; how exact they have to be, the bound alone decides.
No kernel may reach another device: no remote copies, remote signals or barrier semaphores. Data moves between devices by JAX's collectives and lax.ppermute only.
A program may use at most 128 MiB of HBM per device.

v0:
```python
import math
import jax
import jax.numpy as jnp
from jax import lax
from jax.sharding import PartitionSpec as P

LS = 5
SR = 4
LCUT = 1600
BLOCK = 16
DRIFT = 128
ALPHA = math.sqrt(math.log(2.0) / math.pi)
SPACING = 0.5
EPSILON = 1e-06
HIGHEST = lax.Precision.HIGHEST


def with_halo(value, sides, width):
    for axis, dim in sides:
        count, length = (lax.axis_size(axis), value.shape[dim])
        up = [(i, (i + 1) % count) for i in range(count - 1)]
        down = [(j, i) for i, j in up]
        last = lax.slice_in_dim(value, length - width, length, axis=dim)
        leading = lax.slice_in_dim(value, 0, width, axis=dim)
        before = lax.ppermute(last, axis, up)
        after = lax.ppermute(leading, axis, down)
        value = jnp.concatenate([before, value, after], axis=dim)
    return value


def cubic_weights(fraction):
    position = fraction.astype(jnp.float32) / 256.0
    square = position * position
    cube_term = square * position
    return (
        0.5 * (2.0 * square - cube_term - position),
        0.5 * (3.0 * cube_term - 5.0 * square + 2.0),
        0.5 * (4.0 * square - 3.0 * cube_term + position),
        0.5 * (cube_term - square),
    )


def interpolate(window, row_taps, col_taps):
    height = window.shape[0] - 3
    length = window.shape[1] - 3
    across = (
        row_taps[0] * window[0:height]
        + row_taps[1] * window[1 : height + 1]
        + row_taps[2] * window[2 : height + 2]
        + row_taps[3] * window[3 : height + 3]
    )
    return (
        col_taps[0] * across[:, 0:length]
        + col_taps[1] * across[:, 1 : length + 1]
        + col_taps[2] * across[:, 2 : length + 2]
        + col_taps[3] * across[:, 3 : length + 3]
    )


def resample(after_scan, drift_offsets, drift_fractions):
    height, length = (after_scan.shape[1], after_scan.shape[2])
    margin = DRIFT + 2
    widened = with_halo(after_scan, (("row", 1), ("col", 2)), margin)
    row_taps = jnp.stack(cubic_weights(drift_fractions[0, :, 0, 0]), axis=-1)
    col_taps = jnp.stack(cubic_weights(drift_fractions[1, :, 0, 0]), axis=-1)

    def one_scan(window, row_shift, col_shift, row_weights, col_weights):
        source = lax.dynamic_slice(
            window, (margin - 1 + row_shift, margin - 1 + col_shift), (height + 3, length + 3)
        )
        return interpolate(source, row_weights, col_weights)

    return jax.vmap(one_scan)(
        widened, drift_offsets[0, :, 0, 0], drift_offsets[1, :, 0, 0], row_taps, col_taps
    )


def short_taps():
    return [math.exp(-math.pi * (offset / (ALPHA * LS)) ** 2) for offset in range(-SR, SR + 1)]


def short_filter(widened, height, length):
    kernel_taps = short_taps()
    column_index = (
        lax.axis_index("col") * length - SR + jnp.arange(length + 2 * SR, dtype=jnp.int32)
    )
    column_inside = ((column_index >= 0) & (column_index < length * lax.axis_size("col"))).astype(
        jnp.float32
    )
    summed = kernel_taps[0] * widened[:, :, 0:length]
    weight = kernel_taps[0] * column_inside[0:length]
    for offset in range(1, 2 * SR + 1):
        summed = summed + kernel_taps[offset] * widened[:, :, offset : offset + length]
        weight = weight + kernel_taps[offset] * column_inside[offset : offset + length]
    across = summed / weight
    row_index = lax.axis_index("row") * height - SR + jnp.arange(height + 2 * SR, dtype=jnp.int32)
    row_inside = ((row_index >= 0) & (row_index < height * lax.axis_size("row"))).astype(
        jnp.float32
    )
    summed = kernel_taps[0] * across[:, 0:height, :]
    weight = kernel_taps[0] * row_inside[0:height]
    for offset in range(1, 2 * SR + 1):
        summed = summed + kernel_taps[offset] * across[:, offset : offset + height, :]
        weight = weight + kernel_taps[offset] * row_inside[offset : offset + height]
    return summed / weight[:, None]


def coarse_means(surface):
    scans, height, length = surface.shape
    return surface.reshape(scans, height // BLOCK, BLOCK, length // BLOCK, BLOCK).mean(axis=(2, 4))


def gauss_block(source, target):
    distance = ((source[:, None] - target[None, :]) * BLOCK).astype(jnp.float32) / (ALPHA * LCUT)
    return jnp.exp(-math.pi * distance * distance)


def long_cols(coarse):
    width = coarse.shape[2]
    target = lax.axis_index("col") * width + jnp.arange(width, dtype=jnp.int32)
    portion = lax.all_gather(coarse, "col", axis=2, tiled=True)
    source = jnp.arange(portion.shape[2], dtype=jnp.int32)
    matrix = gauss_block(source, target)
    summed = jnp.einsum("frk,kc->frc", portion, matrix, precision=HIGHEST)
    weight = jnp.sum(matrix, axis=0)
    return summed / weight


def long_rows(surface):
    rows_here = surface.shape[1]
    target = lax.axis_index("row") * rows_here + jnp.arange(rows_here, dtype=jnp.int32)
    portion = lax.all_gather(surface, "row", axis=1, tiled=True)
    source = jnp.arange(portion.shape[1], dtype=jnp.int32)
    matrix = gauss_block(target, source)
    summed = jnp.einsum("rk,fkc->frc", matrix, portion, precision=HIGHEST)
    weight = jnp.sum(matrix, axis=1)
    return summed / weight[:, None]


def upsample_matrix(fine_index, coarse_index, coarse_count):
    numerator = 2 * fine_index + 1 - BLOCK
    lower_index = numerator // (2 * BLOCK)
    fraction = (numerator - lower_index * (2 * BLOCK)).astype(jnp.float32) / (2.0 * BLOCK)
    outside = (lower_index < 0) | (lower_index >= coarse_count - 1)
    fraction = jnp.where(outside, jnp.zeros_like(fraction), fraction)
    lower_index = jnp.clip(lower_index, 0, coarse_count - 1)
    first_part = (coarse_index[None, :] == lower_index[:, None]).astype(jnp.float32) * (
        1.0 - fraction
    )[:, None]
    second_part = (coarse_index[None, :] == (lower_index + 1)[:, None]).astype(
        jnp.float32
    ) * fraction[:, None]
    return first_part + second_part


def upsample(wavy_coarse, height, length):
    coarse_rows, coarse_cols = (wavy_coarse.shape[1], wavy_coarse.shape[2])
    widened_coarse = with_halo(wavy_coarse, (("row", 1), ("col", 2)), 1)
    row_fine = lax.axis_index("row") * height + jnp.arange(height, dtype=jnp.int32)
    row_blocks = (
        lax.axis_index("row") * coarse_rows - 1 + jnp.arange(coarse_rows + 2, dtype=jnp.int32)
    )
    col_fine = lax.axis_index("col") * length + jnp.arange(length, dtype=jnp.int32)
    col_blocks = (
        lax.axis_index("col") * coarse_cols - 1 + jnp.arange(coarse_cols + 2, dtype=jnp.int32)
    )
    row_up = upsample_matrix(row_fine, row_blocks, coarse_rows * lax.axis_size("row"))
    col_up = upsample_matrix(col_fine, col_blocks, coarse_cols * lax.axis_size("col"))
    row_mixed = jnp.einsum("pa,sab->spb", row_up, widened_coarse, precision=HIGHEST)
    return jnp.einsum("spb,qb->spq", row_mixed, col_up, precision=HIGHEST)


def slopes(surface):
    height, length = (surface.shape[1], surface.shape[2])
    bordered = with_halo(surface, (("row", 1), ("col", 2)), 1)
    column_index = lax.axis_index("col") * length + jnp.arange(length, dtype=jnp.int32)
    row_index = lax.axis_index("row") * height + jnp.arange(height, dtype=jnp.int32)
    column_mask = (
        (column_index >= 1) & (column_index <= length * lax.axis_size("col") - 2)
    ).astype(jnp.float32)
    row_mask = ((row_index >= 1) & (row_index <= height * lax.axis_size("row") - 2)).astype(
        jnp.float32
    )
    along_cols = (bordered[:, 1:-1, 2:] - bordered[:, 1:-1, :-2]) / (2.0 * SPACING) * column_mask
    along_rows = (
        (bordered[:, 2:, 1:-1] - bordered[:, :-2, 1:-1]) / (2.0 * SPACING) * row_mask[:, None]
    )
    return along_cols * along_cols + along_rows * along_rows


def body(before_scan, after_scan, drift_offsets, drift_fractions):
    height, length = (before_scan.shape[1], before_scan.shape[2])
    shifted = resample(after_scan, drift_offsets, drift_fractions)
    difference = before_scan - shifted
    widened = with_halo(difference, (("row", 1), ("col", 2)), SR)
    smooth = short_filter(widened, height, length)
    coarse = coarse_means(smooth)
    wavy_coarse = long_rows(long_cols(coarse))
    waviness = upsample(wavy_coarse, height, length)
    band_field = smooth - waviness
    slope_field = slopes(band_field)
    height_sq = jnp.sum(band_field * band_field, axis=(1, 2))
    slope_sum = jnp.sum(slope_field, axis=(1, 2))
    height_all, slope_all = lax.psum((height_sq, slope_sum), ("row", "col"))
    total_cells = height * lax.axis_size("row") * length * lax.axis_size("col")
    surface_params = jnp.sqrt(jnp.stack([height_all, slope_all]) / total_cells + EPSILON)
    return (band_field, slope_field, surface_params)


def solution(mesh):
    in_specs = (
        P(None, "row", "col"),
        P(None, "row", "col"),
        P(None, None, "row", "col"),
        P(None, None, "row", "col"),
    )
    out_specs = (P(None, "row", "col"), P(None, "row", "col"), P())
    return jax.shard_map(body, mesh=mesh, in_specs=in_specs, out_specs=out_specs, check_vma=False)
```

profile of v0, /device:TPU:1, one launch (start us, length us, event | category | flops | bytes accessed | tf_op | source)
XLA Modules:
  0.0 455.7 jit_solution(10664465496469987918)
XLA Ops:
  0.6 3.2 fusion.118
  5.3 4.5 collective-permute-start
  9.8 2.7 copy.43
  12.5 2.0 collective-permute-start.1
  14.5 5.2 %copy.28 = f32[4,256,1024]{1,0,2:T(4,128)} copy(f32[4,256,1024]{2,1,0:T(8,128)} %param.5) | data formatting | bytes 8388608 | tf_op args[1]
  19.9 13.1 %collective-permute-done = f32[4,130,1024]{2,0,1:T(4,128)} collective-permute-done((f32[4,130,1024]{2,0,1:T(4,128)S(1)}, f32[4,130,1024]{2,0,1:T(4,128)}, u32[]{:S(2)}, u32[]{:S(2)}) %collective-permute-start) | collective-permute-done | bytes 2129952 | tf_op jit(solution)/shard_map/ppermute | solution.py:25
  33.1 6.2 %copy.27 = f32[4,130,1024]{1,0,2:T(4,128)} copy(f32[4,130,1024]{2,0,1:T(4,128)} %collective-permute-done) | data formatting | bytes 4259840 | tf_op jit(solution)/shard_map/ppermute | solution.py:25
  40.6 6.2 %copy.29 = f32[4,130,1024]{1,0,2:T(4,128)} copy(f32[4,130,1024]{2,0,1:T(4,128)} %collective-permute-done.1) | data formatting | bytes 4259840 | tf_op jit(solution)/shard_map/ppermute | solution.py:26
  46.8 3.5 pad_maximum_fusion.13
  50.3 3.8 collective-permute-start.2
  54.1 1.5 collective-permute-start.3
  56.2 40.7 %collective-permute-done.2 = f32[4,516,130]{1,0,2:T(4,128)S(1)} collective-permute-done((f32[4,516,130]{1,0,2:T(4,128)S(1)}, f32[4,516,130]{1,0,2:T(4,128)S(1)}, u32[]{:S(2)}, u32[]{:S(2)}) %collective-permute-start.2) | collective-permute-done | bytes 1073312 | tf_op jit(solution)/shard_map/ppermute | solution.py:25
  97.0 29.5 %pad_maximum_fusion = f32[4,516,1284]{1,0,2:T(4,128)} fusion(f32[4,516,130]{1,0,2:T(4,128)S(1)} %collective-permute-done.3, f32[4,130,1024]{1,0,2:T(4,128)} %copy.29, f32[4,256,1024]{1,0,2:T(4,128)S(1)} %copy-done.2, f32[4,130,1024]{1,0,2:T(4,128)} %copy.27, f32[4,516,130]{1,0,2:T(4,128)S(1)} %collective-permute-done.2), kind=kLoop, calls=%fused_computation.2 | loop fusion | flops 10600704 | bytes 21201408 | tf_op jit(solution)/shard_map/concatenate | solution.py:27
  126.4 15.3 %copy.30 = f32[4,516,1284]{2,1,0:T(8,128)} copy(f32[4,516,1284]{1,0,2:T(4,128)} %pad_maximum_fusion) | data formatting | bytes 21201408
  141.7 21.6 %while.1 = (s32[]{:T(128)}, f32[4,516,1284]{2,1,0:T(8,128)}, s32[4,3]{1,0:T(4,128)S(1)}, f32[4,259,1027]{2,1,0:T(8,128)}, s32[]{:T(128)}) while((s32[]{:T(128)}, f32[4,516,1284]{2,1,0:T(8,128)}, s32[4,3]{1,0:T(4,128)S(1)}, f32[4,259,1027]{2,1,0:T(8,128)}, s32[]{:T(128)}) %tuple.51), condition=%wide.while_cond, body=%wide.while_body.sunk | while | flops 2 | bytes 2435185 | solution.py:68
  142.3 4.8 %dynamic-slice_dynamic-update-slice_fusion.2 = f32[4,259,1027]{2,1,0:T(8,128)} fusion(f32[4,259,1027]{2,1,0:T(8,128)} %get-tuple-element.118, s32[]{:T(128)} %get-tuple-element.115, f32[4,516,1284]{2,1,0:T(8,128)} %get-tuple-element.121, s32[]{:T(128)} %bitcast.84, s32[]{:T(128)} %bitcast.85, s32[]{:T(128)} %bitcast.86), kind=kLoop, calls=%fused_computation.clone.1 | loop fusion | bytes 2435072 | tf_op jit(solution)/shard_map/vmap()/gather
  147.8 4.7 %dynamic-slice_dynamic-update-slice_fusion.2 = f32[4,259,1027]{2,1,0:T(8,128)} fusion(f32[4,259,1027]{2,1,0:T(8,128)} %get-tuple-element.118, s32[]{:T(128)} %get-tuple-element.115, f32[4,516,1284]{2,1,0:T(8,128)} %get-tuple-element.121, s32[]{:T(128)} %bitcast.84, s32[]{:T(128)} %bitcast.85, s32[]{:T(128)} %bitcast.86), kind=kLoop, calls=%fused_computation.clone.1 | loop fusion | bytes 2435072 | tf_op jit(solution)/shard_map/vmap()/gather
  153.1 4.7 %dynamic-slice_dynamic-update-slice_fusion.2 = f32[4,259,1027]{2,1,0:T(8,128)} fusion(f32[4,259,1027]{2,1,0:T(8,128)} %get-tuple-element.118, s32[]{:T(128)} %get-tuple-element.115, f32[4,516,1284]{2,1,0:T(8,128)} %get-tuple-element.121, s32[]{:T(128)} %bitcast.84, s32[]{:T(128)} %bitcast.85, s32[]{:T(128)} %bitcast.86), kind=kLoop, calls=%fused_computation.clone.1 | loop fusion | bytes 2435072 | tf_op jit(solution)/shard_map/vmap()/gather
  158.5 4.7 %dynamic-slice_dynamic-update-slice_fusion.2 = f32[4,259,1027]{2,1,0:T(8,128)} fusion(f32[4,259,1027]{2,1,0:T(8,128)} %get-tuple-element.118, s32[]{:T(128)} %get-tuple-element.115, f32[4,516,1284]{2,1,0:T(8,128)} %get-tuple-element.121, s32[]{:T(128)} %bitcast.84, s32[]{:T(128)} %bitcast.85, s32[]{:T(128)} %bitcast.86), kind=kLoop, calls=%fused_computation.clone.1 | loop fusion | bytes 2435072 | tf_op jit(solution)/shard_map/vmap()/gather
  163.2 9.2 %multiply_add_fusion = f32[4,256,1027]{2,1,0:T(8,128)S(1)} fusion(f32[4,259,1027]{2,1,0:T(8,128)} %get-tuple-element.10, f32[4]{0:T(128)S(1)} %get-tuple-element.67, f32[4]{0:T(128)S(1)} %get-tuple-element.62, f32[4]{0:T(128)S(1)} %get-tuple-element.64, f32[4]{0:T(128)S(1)} %get-tuple-element.63), kind=kLoop, calls=%fused_computation.5 | loop fusion | flops 7361536 | bytes 21033024 | tf_op jit(solution)/shard_map/vmap()/add | solution.py:47
  172.5 3.4 fusion.25
  176.0 17.8 %collective-permute-start.4 = (f32[4,4,1024]{2,1,0:T(4,128)S(1)}, f32[4,4,1024]{2,1,0:T(4,128)S(1)}, u32[]{:S(2)}, u32[]{:S(2)}) collective-permute-start(f32[4,4,1024]{2,1,0:T(4,128)S(1)} %get-tuple-element.53), channel_id=1, source_target_pairs={{0,8},{8,16},{16,24},{24,32},{32,40},{40,48},{48,56},{56,64},{64,7... | collective-permute-start | bytes 196616 | tf_op jit(solution)/shard_map/ppermute | solution.py:25
  193.8 1.9 collective-permute-start.5
  195.8 3.6 collective-permute-done.5
  200.4 4.1 collective-permute-start.6
  204.8 1.5 collective-permute-start.7
  206.6 3.0 collective-permute-done.7
  209.9 7.4 %maximum_maximum_fusion = (f32[4,264,1028]{2,1,0:T(8,128)S(1)}, f32[4,264,1028]{2,1,0:T(8,128)}) fusion(f32[4,4,1024]{2,1,0:T(4,128)S(1)} %collective-permute-done.5, f32[4,256,1024]{2,1,0:T(8,128)} %copy-done, f32[4,4,1024]{2,1,0:T(4,128)S(1)} %collective-permute-done.4, f32[4,264,4]{2,1,0:T(8,128)S(1)} %copy.33, f32[4,264,4]{2,1,0:T(8,128)S(1)} %copy.35), kind=kLoop, calls=%fused_computation.3 | loop fusion | flops 6513408 | bytes 13043712 | tf_op jit(solution)/shard_map/concatenate | solution.py:27
  217.3 15.3 %fusion.1 = f32[4,264,1024]{2,1,0:T(8,128)S(1)} fusion(f32[4,264,1028]{2,1,0:T(8,128)} %get-tuple-element.45, f32[4,264,1028]{2,1,0:T(8,128)S(1)} %get-tuple-element.44, f32[1024]{0:T(1024)S(1)} %fusion.80, f32[4,4,1024]{2,1,0:T(4,128)S(1)} %collective-permute-done.5, f32[4,256,1024]{2,1,0:T(8,128)} %copy-done, f32[4,4,1024]{2,1,0:T(4,128)S(1)} %collective-permute-done.4), kind=kLoop, calls=%fused_computation.8 | loop fusion | flops 20545536 | bytes 43257856 | tf_op jit(solution)/shard_map/div | solution.py:95
  232.7 5.7 %fusion.17 = f32[4,256,1024]{2,1,0:T(8,128)} fusion(f32[4,264,1024]{2,1,0:T(8,128)S(1)} %fusion.1, f32[256]{0:T(256)S(1)} %multiply_add_fusion.3), kind=kLoop, calls=%fused_computation.41 | loop fusion | flops 17825792 | bytes 41944064 | tf_op jit(solution)/shard_map/div | solution.py:105
  238.3 19.0 %reshape.249 = f32[4,16,16,64,16]{4,3,2,1,0:T(8,128)} reshape(f32[4,256,1024]{2,1,0:T(8,128)} %fusion.17) | data formatting | bytes 8388608 | tf_op jit(solution)/shard_map/reshape | solution.py:110
  257.3 12.2 %reduce_sum.45 = f32[4,16,64]{2,1,0:T(8,128)S(1)} reduce(f32[4,16,16,64,16]{4,3,2,1,0:T(8,128)} %reshape.249, f32[]{:T(128)} %constant.64.clone.1), dimensions={2,4}, to_apply=%region_0.0 | reduce | flops 1044480 | bytes 4210692 | tf_op jit(solution)/shard_map/reduce_sum | solution.py:110
  269.6 27.9 %all_gather.6 = f32[4,16,512]{1,0,2:T(4,128)S(1)} all-gather(f32[4,16,64]{1,0,2:T(4,128)S(1)} %copy.36), channel_id=1, replica_groups=mesh['row'=16,'col'=8] {'col'}, dimensions={2}, use_global_device_ids=true | all-gather | bytes 147456 | tf_op jit(solution)/shard_map/all_gather | solution.py:121
  297.5 1.8 convolution_divide_fusion
  299.3 27.6 %all_gather.7 = f32[4,256,64]{2,1,0:T(8,128)S(1)} all-gather(f32[4,16,64]{2,1,0:T(8,128)S(1)} %convolution_divide_fusion), channel_id=1, replica_groups=mesh['row'=16,'col'=8] {'row'}, dimensions={1}, use_global_device_ids=true | all-gather | bytes 278528 | tf_op jit(solution)/shard_map/all_gather | solution.py:132
  327.3 1.9 collective-permute-start.8
  329.3 2.4 collective-permute-start.9
  331.7 2.5 collective-permute-done.9
  334.3 1.8 collective-permute-start.10
  336.1 1.6 collective-permute-start.11
  337.7 3.2 collective-permute-done.11
  341.5 6.0 %convolution_subtract_fusion = f32[4,256,1024]{2,1,0:T(8,128)S(1)} fusion(f32[4,256,1024]{2,1,0:T(8,128)} %fusion.17, f32[4,256,66]{1,2,0:T(8,128)S(1)} %convolution_bitcast_fusion, f32[1024]{0:T(1024)S(1)} %get-tuple-element.71, s32[1024]{0:T(1024)S(1)} %get-tuple-element.74, f32[1024]{0:T(1024)S(1)} %get-tuple-element.72, ...), kind=kOutput, calls=%fused_computation.65 | convolution fusion | flops 831858688 | bytes 8675592 | tf_op jit(solution)/shard_map/spb,qb->spq/dot_general | solution.py:170
  347.5 3.4 collective-permute-start.12
  350.9 1.9 collective-permute-start.13
  352.9 3.1 collective-permute-done.13
  358.1 4.0 collective-permute-start.15
  363.0 13.9 %fusion.112 = (f32[4]{0:T(128)S(1)}, f32[4,256,1024]{2,1,0:T(8,128)}, f32[4]{0:T(128)S(1)}) fusion(f32[256]{0:T(256)S(1)} %and_convert_fusion, f32[4,256,1024]{2,1,0:T(8,128)} %copy-done.1, f32[4,1,1024]{2,1,0:T(1,128)S(1)} %collective-permute-done.12, f32[4,1,1024]{2,1,0:T(1,128)S(1)} %collective-permute-done.13, f32[1024]{0:T(1024)S(1)} %fusion.92, ...), kind=kLoop, calls=%fused_computation.219 | loop fusion | flops 18874360 | bytes 8434784 | tf_op jit(solution)/shard_map/reduce_sum | solution.py:203
  377.0 78.1 %all-reduce = (f32[1,4]{1,0:T(1,128)S(1)}, f32[1,4]{1,0:T(1,128)S(1)}) all-reduce(f32[1,4]{1,0:T(1,128)S(1)} %bitcast.87, f32[1,4]{1,0:T(1,128)S(1)} %bitcast.88), channel_id=1, replica_groups=mesh['row'=16,'col'=8] {'row','col'}, use_global_device_ids=true, to_apply=%region_6.7 | all-reduce | flops 8 | bytes 64 | tf_op jit(solution)/shard_map/psum | solution.py:204
  (74 shorter events, 12.7 us)
Async XLA Ops:
  5.3 27.8 %collective-permute-start = (f32[4,130,1024]{2,0,1:T(4,128)S(1)}, f32[4,130,1024]{2,0,1:T(4,128)}, u32[]{:S(2)}, u32[]{:S(2)}) collective-permute-start(f32[4,130,1024]{2,0,1:T(4,128)S(1)} %copy.42), channel_id=1, source_target_pairs={{0,8},{8,16},{16,24},{24,32},{32,40},{40,48},{48,56},{56,64},{64,7... | collective-permute-start | bytes 6389768 | tf_op jit(solution)/shard_map/ppermute | solution.py:25
  12.5 7.3 %copy-start.5 = (s32[2,4,1,1]{1,3,2,0:T(1,128)S(1)}, s32[2,4,1,1]{1,3,2,0:T(1,128)}, u32[]{:S(2)}) copy-start(s32[2,4,1,1]{1,3,2,0:T(1,128)} %param.6) | copy-start | bytes 100
  12.5 28.1 %collective-permute-start.1 = (f32[4,130,1024]{2,0,1:T(4,128)}, f32[4,130,1024]{2,0,1:T(4,128)}, u32[]{:S(2)}, u32[]{:S(2)}) collective-permute-start(f32[4,130,1024]{2,0,1:T(4,128)} %copy.43), channel_id=1, source_target_pairs={{8,0},{16,8},{24,16},{32,24},{40,32},{48,40},{56,48},{64,56},{72,6... | collective-permute-start | bytes 6389768 | tf_op jit(solution)/shard_map/ppermute | solution.py:26
  46.8 9.3 %copy-start.4 = (s32[2,4,1,1]{1,3,2,0:T(1,128)S(1)}, s32[2,4,1,1]{1,3,2,0:T(1,128)}, u32[]{:S(2)}) copy-start(s32[2,4,1,1]{1,3,2,0:T(1,128)} %param.7) | copy-start | bytes 100
  46.8 50.1 %copy-start.2 = (f32[4,256,1024]{1,0,2:T(4,128)S(1)}, f32[4,256,1024]{1,0,2:T(4,128)}, u32[]{:S(2)}) copy-start(f32[4,256,1024]{1,0,2:T(4,128)} %copy.28) | copy-start | bytes 12582916
  50.3 46.6 %collective-permute-start.2 = (f32[4,516,130]{1,0,2:T(4,128)S(1)}, f32[4,516,130]{1,0,2:T(4,128)S(1)}, u32[]{:S(2)}, u32[]{:S(2)}) collective-permute-start(f32[4,516,130]{1,0,2:T(4,128)S(1)} %get-tuple-element.42), channel_id=1, source_target_pairs={{0,1},{1,2},{2,3},{3,4},{4,5},{5,6},{6,7},{8,9},{9,10},{10,11},{11... | collective-permute-start | bytes 3219848 | tf_op jit(solution)/shard_map/ppermute | solution.py:25
  54.1 42.8 %collective-permute-start.3 = (f32[4,516,130]{1,0,2:T(4,128)S(1)}, f32[4,516,130]{1,0,2:T(4,128)S(1)}, u32[]{:S(2)}, u32[]{:S(2)}) collective-permute-start(f32[4,516,130]{1,0,2:T(4,128)S(1)} %get-tuple-element.43), channel_id=1, source_target_pairs={{1,0},{2,1},{3,2},{4,3},{5,4},{6,5},{7,6},{9,8},{10,9},{11,10},{12... | collective-permute-start | bytes 3219848 | tf_op jit(solution)/shard_map/ppermute | solution.py:26
  163.2 9.2 %copy-start.3 = (f32[4,256,1024]{2,1,0:T(8,128)S(1)}, f32[4,256,1024]{2,1,0:T(8,128)}, u32[]{:S(2)}) copy-start(f32[4,256,1024]{2,1,0:T(8,128)} %param.4) | copy-start | bytes 12582916
  175.9 24.1 %copy-start = (f32[4,256,1024]{2,1,0:T(8,128)}, f32[4,256,1024]{2,1,0:T(8,128)S(1)}, u32[]{:S(2)}) copy-start(f32[4,256,1024]{2,1,0:T(8,128)S(1)} %fusion.25) | copy-start | bytes 12582916
  176.0 19.8 %collective-permute-start.4 = (f32[4,4,1024]{2,1,0:T(4,128)S(1)}, f32[4,4,1024]{2,1,0:T(4,128)S(1)}, u32[]{:S(2)}, u32[]{:S(2)}) collective-permute-start(f32[4,4,1024]{2,1,0:T(4,128)S(1)} %get-tuple-element.53), channel_id=1, source_target_pairs={{0,8},{8,16},{16,24},{24,32},{32,40},{40,48},{48,56},{56,64},{64,7... | collective-permute-start | bytes 196616 | tf_op jit(solution)/shard_map/ppermute | solution.py:25
  193.8 5.6 %collective-permute-start.5 = (f32[4,4,1024]{2,1,0:T(4,128)S(1)}, f32[4,4,1024]{2,1,0:T(4,128)S(1)}, u32[]{:S(2)}, u32[]{:S(2)}) collective-permute-start(f32[4,4,1024]{2,1,0:T(4,128)S(1)} %get-tuple-element.54), channel_id=1, source_target_pairs={{8,0},{16,8},{24,16},{32,24},{40,32},{48,40},{56,48},{64,56},{72,6... | collective-permute-start | bytes 196616 | tf_op jit(solution)/shard_map/ppermute | solution.py:26
  200.4 5.9 %collective-permute-start.6 = (f32[4,264,4]{1,2,0:T(4,128)S(1)}, f32[4,264,4]{1,2,0:T(4,128)S(1)}, u32[]{:S(2)}, u32[]{:S(2)}) collective-permute-start(f32[4,264,4]{1,2,0:T(4,128)S(1)} %copy.32), channel_id=1, source_target_pairs={{0,1},{1,2},{2,3},{3,4},{4,5},{5,6},{6,7},{8,9},{9,10},{10,11},{11... | collective-permute-start | bytes 50696 | tf_op jit(solution)/shard_map/ppermute | solution.py:25
  204.8 4.8 %collective-permute-start.7 = (f32[4,264,4]{1,2,0:T(4,128)S(1)}, f32[4,264,4]{1,2,0:T(4,128)S(1)}, u32[]{:S(2)}, u32[]{:S(2)}) collective-permute-start(f32[4,264,4]{1,2,0:T(4,128)S(1)} %copy.34), channel_id=1, source_target_pairs={{1,0},{2,1},{3,2},{4,3},{5,4},{6,5},{7,6},{9,8},{10,9},{11,10},{12... | collective-permute-start | bytes 50696 | tf_op jit(solution)/shard_map/ppermute | solution.py:26
  327.3 4.4 collective-permute-start.8
  329.3 4.9 %collective-permute-start.9 = (f32[4,1,64]{2,1,0:T(1,128)S(1)}, f32[4,1,64]{2,1,0:T(1,128)S(1)}, u32[]{:S(2)}, u32[]{:S(2)}) collective-permute-start(f32[4,1,64]{2,1,0:T(1,128)S(1)} %get-tuple-element.60), channel_id=1, source_target_pairs={{8,0},{16,8},{24,16},{32,24},{40,32},{48,40},{56,48},{64,56},{72,6... | collective-permute-start | bytes 3080 | tf_op jit(solution)/shard_map/ppermute | solution.py:26
  334.3 3.4 collective-permute-start.10
  336.1 4.8 %collective-permute-start.11 = (f32[4,18,1]{2,1,0:T(8,128)S(1)}, f32[4,18,1]{2,1,0:T(8,128)S(1)}, u32[]{:S(2)}, u32[]{:S(2)}) collective-permute-start(f32[4,18,1]{2,1,0:T(8,128)S(1)} %get-tuple-element.58), channel_id=1, source_target_pairs={{1,0},{2,1},{3,2},{4,3},{5,4},{6,5},{7,6},{9,8},{10,9},{11,10},{12... | collective-permute-start | bytes 872 | tf_op jit(solution)/shard_map/ppermute | solution.py:26
  347.5 8.5 %copy-start.1 = (f32[4,256,1024]{2,1,0:T(8,128)}, f32[4,256,1024]{2,1,0:T(8,128)S(1)}, u32[]{:S(2)}) copy-start(f32[4,256,1024]{2,1,0:T(8,128)S(1)} %convolution_subtract_fusion) | copy-start | bytes 12582916
  347.5 5.3 %collective-permute-start.12 = (f32[4,1,1024]{2,1,0:T(1,128)S(1)}, f32[4,1,1024]{2,1,0:T(1,128)S(1)}, u32[]{:S(2)}, u32[]{:S(2)}) collective-permute-start(f32[4,1,1024]{2,1,0:T(1,128)S(1)} %get-tuple-element.52), channel_id=1, source_target_pairs={{0,8},{8,16},{16,24},{24,32},{32,40},{40,48},{48,56},{56,64},{64,7... | collective-permute-start | bytes 49160 | tf_op jit(solution)/shard_map/ppermute | solution.py:25
  350.9 5.1 %collective-permute-start.13 = (f32[4,1,1024]{2,1,0:T(1,128)S(1)}, f32[4,1,1024]{2,1,0:T(1,128)S(1)}, u32[]{:S(2)}, u32[]{:S(2)}) collective-permute-start(f32[4,1,1024]{2,1,0:T(1,128)S(1)} %get-tuple-element.51), channel_id=1, source_target_pairs={{8,0},{16,8},{24,16},{32,24},{40,32},{48,40},{56,48},{64,56},{72,6... | collective-permute-start | bytes 49160 | tf_op jit(solution)/shard_map/ppermute | solution.py:26
  356.5 5.6 %collective-permute-start.14 = (f32[4,258,1]{1,0,2:T(4,128)S(1)}, f32[4,258,1]{1,0,2:T(4,128)S(1)}, u32[]{:S(2)}, u32[]{:S(2)}) collective-permute-start(f32[4,258,1]{1,0,2:T(4,128)S(1)} %copy.38), channel_id=1, source_target_pairs={{1,0},{2,1},{3,2},{4,3},{5,4},{6,5},{7,6},{9,8},{10,9},{11,10},{12... | collective-permute-start | bytes 12392 | tf_op jit(solution)/shard_map/ppermute | solution.py:26
  358.1 4.8 %collective-permute-start.15 = (f32[4,258,1]{1,0,2:T(4,128)S(1)}, f32[4,258,1]{1,0,2:T(4,128)S(1)}, u32[]{:S(2)}, u32[]{:S(2)}) collective-permute-start(f32[4,258,1]{1,0,2:T(4,128)S(1)} %copy.40), channel_id=1, source_target_pairs={{0,1},{1,2},{2,3},{3,4},{4,5},{5,6},{6,7},{8,9},{9,10},{10,11},{11... | collective-permute-start | bytes 12392 | tf_op jit(solution)/shard_map/ppermute | solution.py:25
where the time goes:
time: 458 us; the launch traced here: 456 us
  blocking collectives  134 us (29%)
  other arithmetic  102 us (22%)
  local copies, waits for them, and re-layouts  83.4 us (18%)
  waiting for transfers between devices  71.2 us (16%)
  starting transfers between devices  55.5 us (12%)
  matrix products  8.74 us (2%)
    psum x1, blocking collectives, body(): height_all, slope_all = lax.psum((height_sq, slope_sum), ('row', 'col'))  78.1 us
    ppermute x8, waiting for transfers between devices, with_halo(): before = lax.ppermute(last, axis, up)  54.4 us
    ppermute x8, starting transfers between devices, with_halo(): before = lax.ppermute(last, axis, up)  41.4 us
    concatenate x4, other arithmetic, with_halo(): value = jnp.concatenate([before, value, after], axis=dim)  37.5 us
    all_gather x1, blocking collectives, long_cols(): portion = lax.all_gather(coarse, 'col', axis=2, tiled=True)  27.9 us
    all_gather x1, blocking collectives, long_rows(): portion = lax.all_gather(surface, 'row', axis=1, tiled=True)  27.6 us
    unnamed x18, local copies, waits for them, and re-layouts  24.7 us
    gather x12, local copies, waits for them, and re-layouts  21.5 us
  transfers between devices with their start and end apart: 16, of which 9 were waited for; matrix products, arithmetic and copies ran while one was open for 4% of the time, Pallas kernels for 0%

commit v1 on v0

--- a/solution.py
+++ b/solution.py
@@ -201,7 +201,7 @@
     slope_field = slopes(band_field)
     height_sq = jnp.sum(band_field * band_field, axis=(1, 2))
     slope_sum = jnp.sum(slope_field, axis=(1, 2))
-    height_all, slope_all = lax.psum((height_sq, slope_sum), ("row", "col"))
+    height_all, slope_all = lax.psum(lax.psum((height_sq, slope_sum), "col"), "row")
     total_cells = height * lax.axis_size("row") * length * lax.axis_size("col")
     surface_params = jnp.sqrt(jnp.stack([height_all, slope_all]) / total_cells + EPSILON)
     return (band_field, slope_field, surface_params)

time: 458 us -> 441 us (0.963)
  the two profiles are of different devices: /device:TPU:1 before, /device:TPU:65 now
where the time goes in v1:
time: 441 us; the launch traced here: 439 us
  blocking collectives  116 us (26%)
  other arithmetic  102 us (23%)
  local copies, waits for them, and re-layouts  83.1 us (19%)
  waiting for transfers between devices  80.5 us (18%)
  starting transfers between devices  46.7 us (11%)
  matrix products  8.74 us (2%)
    ppermute x8, waiting for transfers between devices, with_halo(): before = lax.ppermute(last, axis, up)  64.9 us
    psum x1, blocking collectives, body(): lax.psum(lax.psum((height_sq, slope_sum), 'col'), 'row')  43 us
    concatenate x4, other arithmetic, with_halo(): value = jnp.concatenate([before, value, after], axis=dim)  37.5 us
    ppermute x8, starting transfers between devices, with_halo(): before = lax.ppermute(last, axis, up)  30.9 us
    all_gather x1, blocking collectives, long_rows(): portion = lax.all_gather(surface, 'row', axis=1, tiled=True)  28.7 us
    all_gather x1, blocking collectives, long_cols(): portion = lax.all_gather(coarse, 'col', axis=2, tiled=True)  28 us
    unnamed x18, local copies, waits for them, and re-layouts  24.7 us
    gather x12, local copies, waits for them, and re-layouts  21.3 us
  transfers between devices with their start and end apart: 16, of which 9 were waited for; matrix products, arithmetic and copies ran while one was open for 4% of the time, Pallas kernels for 0%

profile of v1, /device:TPU:65, one launch (start us, length us, event | category | flops | bytes accessed | tf_op | source)
XLA Modules:
  0.0 438.7 jit_solution(10818376097326824625)
XLA Ops:
  0.6 3.2 fusion.118
  3.9 1.4 copy.42
  5.3 3.7 collective-permute-start
  8.9 2.7 copy.43
  11.7 2.0 collective-permute-start.1
  13.7 5.2 %copy.28 = f32[4,256,1024]{1,0,2:T(4,128)} copy(f32[4,256,1024]{2,1,0:T(8,128)} %param.5) | data formatting | bytes 8388608 | tf_op args[1]
  19.1 13.1 %collective-permute-done = f32[4,130,1024]{2,0,1:T(4,128)} collective-permute-done((f32[4,130,1024]{2,0,1:T(4,128)S(1)}, f32[4,130,1024]{2,0,1:T(4,128)}, u32[]{:S(2)}, u32[]{:S(2)}) %collective-permute-start) | collective-permute-done | bytes 2129952 | tf_op jit(solution)/shard_map/ppermute | solution.py:25
  32.3 6.3 %copy.27 = f32[4,130,1024]{1,0,2:T(4,128)} copy(f32[4,130,1024]{2,0,1:T(4,128)} %collective-permute-done) | data formatting | bytes 4259840 | tf_op jit(solution)/shard_map/ppermute | solution.py:25
  39.8 6.2 %copy.29 = f32[4,130,1024]{1,0,2:T(4,128)} copy(f32[4,130,1024]{2,0,1:T(4,128)} %collective-permute-done.1) | data formatting | bytes 4259840 | tf_op jit(solution)/shard_map/ppermute | solution.py:26
  46.0 3.5 pad_maximum_fusion.13
  49.5 3.3 collective-permute-start.2
  52.8 1.5 collective-permute-start.3
  54.9 51.2 %collective-permute-done.2 = f32[4,516,130]{1,0,2:T(4,128)S(1)} collective-permute-done((f32[4,516,130]{1,0,2:T(4,128)S(1)}, f32[4,516,130]{1,0,2:T(4,128)S(1)}, u32[]{:S(2)}, u32[]{:S(2)}) %collective-permute-start.2) | collective-permute-done | bytes 1073312 | tf_op jit(solution)/shard_map/ppermute | solution.py:25
  106.2 29.5 %pad_maximum_fusion = f32[4,516,1284]{1,0,2:T(4,128)} fusion(f32[4,516,130]{1,0,2:T(4,128)S(1)} %collective-permute-done.3, f32[4,130,1024]{1,0,2:T(4,128)} %copy.29, f32[4,256,1024]{1,0,2:T(4,128)S(1)} %copy-done.2, f32[4,130,1024]{1,0,2:T(4,128)} %copy.27, f32[4,516,130]{1,0,2:T(4,128)S(1)} %collective-permute-done.2), kind=kLoop, calls=%fused_computation.2 | loop fusion | flops 10600704 | bytes 21201408 | tf_op jit(solution)/shard_map/concatenate | solution.py:27
  135.6 15.3 %copy.30 = f32[4,516,1284]{2,1,0:T(8,128)} copy(f32[4,516,1284]{1,0,2:T(4,128)} %pad_maximum_fusion) | data formatting | bytes 21201408
  150.9 21.3 %while.1 = (s32[]{:T(128)}, f32[4,516,1284]{2,1,0:T(8,128)}, s32[4,3]{1,0:T(4,128)S(1)}, f32[4,259,1027]{2,1,0:T(8,128)}, s32[]{:T(128)}) while((s32[]{:T(128)}, f32[4,516,1284]{2,1,0:T(8,128)}, s32[4,3]{1,0:T(4,128)S(1)}, f32[4,259,1027]{2,1,0:T(8,128)}, s32[]{:T(128)}) %tuple.51), condition=%wide.while_cond, body=%wide.while_body.sunk | while | flops 2 | bytes 2435185 | solution.py:68
  151.5 4.8 %dynamic-slice_dynamic-update-slice_fusion.2 = f32[4,259,1027]{2,1,0:T(8,128)} fusion(f32[4,259,1027]{2,1,0:T(8,128)} %get-tuple-element.120, s32[]{:T(128)} %get-tuple-element.117, f32[4,516,1284]{2,1,0:T(8,128)} %get-tuple-element.123, s32[]{:T(128)} %bitcast.84, s32[]{:T(128)} %bitcast.85, s32[]{:T(128)} %bitcast.86), kind=kLoop, calls=%fused_computation.clone.1 | loop fusion | bytes 2435072 | tf_op jit(solution)/shard_map/vmap()/gather
  156.9 4.7 %dynamic-slice_dynamic-update-slice_fusion.2 = f32[4,259,1027]{2,1,0:T(8,128)} fusion(f32[4,259,1027]{2,1,0:T(8,128)} %get-tuple-element.120, s32[]{:T(128)} %get-tuple-element.117, f32[4,516,1284]{2,1,0:T(8,128)} %get-tuple-element.123, s32[]{:T(128)} %bitcast.84, s32[]{:T(128)} %bitcast.85, s32[]{:T(128)} %bitcast.86), kind=kLoop, calls=%fused_computation.clone.1 | loop fusion | bytes 2435072 | tf_op jit(solution)/shard_map/vmap()/gather
  162.2 4.7 %dynamic-slice_dynamic-update-slice_fusion.2 = f32[4,259,1027]{2,1,0:T(8,128)} fusion(f32[4,259,1027]{2,1,0:T(8,128)} %get-tuple-element.120, s32[]{:T(128)} %get-tuple-element.117, f32[4,516,1284]{2,1,0:T(8,128)} %get-tuple-element.123, s32[]{:T(128)} %bitcast.84, s32[]{:T(128)} %bitcast.85, s32[]{:T(128)} %bitcast.86), kind=kLoop, calls=%fused_computation.clone.1 | loop fusion | bytes 2435072 | tf_op jit(solution)/shard_map/vmap()/gather
  167.5 4.7 %dynamic-slice_dynamic-update-slice_fusion.2 = f32[4,259,1027]{2,1,0:T(8,128)} fusion(f32[4,259,1027]{2,1,0:T(8,128)} %get-tuple-element.120, s32[]{:T(128)} %get-tuple-element.117, f32[4,516,1284]{2,1,0:T(8,128)} %get-tuple-element.123, s32[]{:T(128)} %bitcast.84, s32[]{:T(128)} %bitcast.85, s32[]{:T(128)} %bitcast.86), kind=kLoop, calls=%fused_computation.clone.1 | loop fusion | bytes 2435072 | tf_op jit(solution)/shard_map/vmap()/gather
  172.2 9.2 %multiply_add_fusion = f32[4,256,1027]{2,1,0:T(8,128)S(1)} fusion(f32[4,259,1027]{2,1,0:T(8,128)} %get-tuple-element.10, f32[4]{0:T(128)S(1)} %get-tuple-element.69, f32[4]{0:T(128)S(1)} %get-tuple-element.64, f32[4]{0:T(128)S(1)} %get-tuple-element.66, f32[4]{0:T(128)S(1)} %get-tuple-element.65), kind=kLoop, calls=%fused_computation.5 | loop fusion | flops 7361536 | bytes 21033024 | tf_op jit(solution)/shard_map/vmap()/add | solution.py:47
  181.5 3.4 fusion.25
  184.9 7.5 %collective-permute-start.4 = (f32[4,4,1024]{2,1,0:T(4,128)S(1)}, f32[4,4,1024]{2,1,0:T(4,128)S(1)}, u32[]{:S(2)}, u32[]{:S(2)}) collective-permute-start(f32[4,4,1024]{2,1,0:T(4,128)S(1)} %get-tuple-element.55), channel_id=1, source_target_pairs={{0,8},{8,16},{16,24},{24,32},{32,40},{40,48},{48,56},{56,64},{64,7... | collective-permute-start | bytes 196616 | tf_op jit(solution)/shard_map/ppermute | solution.py:25
  192.4 1.9 collective-permute-start.5
  194.4 3.9 collective-permute-done.5
  199.3 4.1 collective-permute-start.6
  203.7 1.5 collective-permute-start.7
  205.5 3.3 collective-permute-done.7
  209.1 7.4 %maximum_maximum_fusion = (f32[4,264,1028]{2,1,0:T(8,128)S(1)}, f32[4,264,1028]{2,1,0:T(8,128)}) fusion(f32[4,4,1024]{2,1,0:T(4,128)S(1)} %collective-permute-done.5, f32[4,256,1024]{2,1,0:T(8,128)} %copy-done, f32[4,4,1024]{2,1,0:T(4,128)S(1)} %collective-permute-done.4, f32[4,264,4]{2,1,0:T(8,128)S(1)} %copy.33, f32[4,264,4]{2,1,0:T(8,128)S(1)} %copy.35), kind=kLoop, calls=%fused_computation.3 | loop fusion | flops 6513408 | bytes 13043712 | tf_op jit(solution)/shard_map/concatenate | solution.py:27
  216.5 15.3 %fusion.1 = f32[4,264,1024]{2,1,0:T(8,128)S(1)} fusion(f32[4,264,1028]{2,1,0:T(8,128)} %get-tuple-element.47, f32[4,264,1028]{2,1,0:T(8,128)S(1)} %get-tuple-element.46, f32[1024]{0:T(1024)S(1)} %fusion.80, f32[4,4,1024]{2,1,0:T(4,128)S(1)} %collective-permute-done.5, f32[4,256,1024]{2,1,0:T(8,128)} %copy-done, f32[4,4,1024]{2,1,0:T(4,128)S(1)} %collective-permute-done.4), kind=kLoop, calls=%fused_computation.8 | loop fusion | flops 20545536 | bytes 43257856 | tf_op jit(solution)/shard_map/div | solution.py:95
  231.8 5.7 %fusion.17 = f32[4,256,1024]{2,1,0:T(8,128)} fusion(f32[4,264,1024]{2,1,0:T(8,128)S(1)} %fusion.1, f32[256]{0:T(256)S(1)} %multiply_add_fusion.3), kind=kLoop, calls=%fused_computation.41 | loop fusion | flops 17825792 | bytes 41944064 | tf_op jit(solution)/shard_map/div | solution.py:105
  237.5 19.0 %reshape.249 = f32[4,16,16,64,16]{4,3,2,1,0:T(8,128)} reshape(f32[4,256,1024]{2,1,0:T(8,128)} %fusion.17) | data formatting | bytes 8388608 | tf_op jit(solution)/shard_map/reshape | solution.py:110
  256.5 12.2 %reduce_sum.45 = f32[4,16,64]{2,1,0:T(8,128)S(1)} reduce(f32[4,16,16,64,16]{4,3,2,1,0:T(8,128)} %reshape.249, f32[]{:T(128)} %constant.64.clone.1), dimensions={2,4}, to_apply=%region_0.0 | reduce | flops 1044480 | bytes 4210692 | tf_op jit(solution)/shard_map/reduce_sum | solution.py:110
  268.8 28.0 %all_gather.6 = f32[4,16,512]{1,0,2:T(4,128)S(1)} all-gather(f32[4,16,64]{1,0,2:T(4,128)S(1)} %copy.36), channel_id=1, replica_groups=mesh['row'=16,'col'=8] {'col'}, dimensions={2}, use_global_device_ids=true | all-gather | bytes 147456 | tf_op jit(solution)/shard_map/all_gather | solution.py:121
  296.8 1.8 convolution_divide_fusion
  298.6 28.7 %all_gather.7 = f32[4,256,64]{2,1,0:T(8,128)S(1)} all-gather(f32[4,16,64]{2,1,0:T(8,128)S(1)} %convolution_divide_fusion), channel_id=1, replica_groups=mesh['row'=16,'col'=8] {'row'}, dimensions={1}, use_global_device_ids=true | all-gather | bytes 278528 | tf_op jit(solution)/shard_map/all_gather | solution.py:132
  327.7 3.5 collective-permute-start.8
  331.2 1.9 collective-permute-start.9
  333.2 3.0 collective-permute-done.9
  337.5 1.6 collective-permute-start.11
  339.1 3.2 collective-permute-done.11
  342.9 6.0 %convolution_subtract_fusion = f32[4,256,1024]{2,1,0:T(8,128)S(1)} fusion(f32[4,256,1024]{2,1,0:T(8,128)} %fusion.17, f32[4,256,66]{1,2,0:T(8,128)S(1)} %convolution_bitcast_fusion, f32[1024]{0:T(1024)S(1)} %get-tuple-element.73, s32[1024]{0:T(1024)S(1)} %get-tuple-element.76, f32[1024]{0:T(1024)S(1)} %get-tuple-element.74, ...), kind=kOutput, calls=%fused_computation.65 | convolution fusion | flops 831858688 | bytes 8675592 | tf_op jit(solution)/shard_map/spb,qb->spq/dot_general | solution.py:170
  349.0 3.1 collective-permute-start.12
  352.1 4.1 collective-permute-start.13
  359.2 4.4 collective-permute-start.15
  364.6 13.9 %fusion.112 = (f32[4]{0:T(128)S(1)}, f32[4,256,1024]{2,1,0:T(8,128)}, f32[4]{0:T(128)S(1)}) fusion(f32[256]{0:T(256)S(1)} %and_convert_fusion, f32[4,256,1024]{2,1,0:T(8,128)} %copy-done.1, f32[4,1,1024]{2,1,0:T(1,128)S(1)} %collective-permute-done.12, f32[4,1,1024]{2,1,0:T(1,128)S(1)} %collective-permute-done.13, f32[1024]{0:T(1024)S(1)} %fusion.92, ...), kind=kLoop, calls=%fused_computation.219 | loop fusion | flops 18874360 | bytes 8434784 | tf_op jit(solution)/shard_map/reduce_sum | solution.py:203
  378.5 16.6 %all-reduce.1 = (f32[4]{0:T(128)S(1)}, f32[4]{0:T(128)S(1)}) all-reduce(f32[4]{0:T(128)S(1)} %get-tuple-element.39, f32[4]{0:T(128)S(1)} %get-tuple-element.52), channel_id=1, replica_groups=mesh['row'=16,'col'=8] {'col'}, use_global_device_ids=true, to_apply=%region_7.8 | all-reduce | flops 8 | bytes 64 | tf_op jit(solution)/shard_map/psum | solution.py:204
  395.1 43.0 %all-reduce = (f32[1,4]{1,0:T(1,128)S(1)}, f32[1,4]{1,0:T(1,128)S(1)}) all-reduce(f32[1,4]{1,0:T(1,128)S(1)} %bitcast.87, f32[1,4]{1,0:T(1,128)S(1)} %bitcast.88), channel_id=1, replica_groups=mesh['row'=16,'col'=8] {'row'}, use_global_device_ids=true, to_apply=%region_8.9 | all-reduce | flops 8 | bytes 64 | tf_op jit(solution)/shard_map/psum | solution.py:204
  (75 shorter events, 13.4 us)
Async XLA Ops:
  5.3 27.0 %collective-permute-start = (f32[4,130,1024]{2,0,1:T(4,128)S(1)}, f32[4,130,1024]{2,0,1:T(4,128)}, u32[]{:S(2)}, u32[]{:S(2)}) collective-permute-start(f32[4,130,1024]{2,0,1:T(4,128)S(1)} %copy.42), channel_id=1, source_target_pairs={{0,8},{8,16},{16,24},{24,32},{32,40},{40,48},{48,56},{56,64},{64,7... | collective-permute-start | bytes 6389768 | tf_op jit(solution)/shard_map/ppermute | solution.py:25
  11.7 7.3 %copy-start.5 = (s32[2,4,1,1]{1,3,2,0:T(1,128)S(1)}, s32[2,4,1,1]{1,3,2,0:T(1,128)}, u32[]{:S(2)}) copy-start(s32[2,4,1,1]{1,3,2,0:T(1,128)} %param.6) | copy-start | bytes 100
  11.7 28.1 %collective-permute-start.1 = (f32[4,130,1024]{2,0,1:T(4,128)}, f32[4,130,1024]{2,0,1:T(4,128)}, u32[]{:S(2)}, u32[]{:S(2)}) collective-permute-start(f32[4,130,1024]{2,0,1:T(4,128)} %copy.43), channel_id=1, source_target_pairs={{8,0},{16,8},{24,16},{32,24},{40,32},{48,40},{56,48},{64,56},{72,6... | collective-permute-start | bytes 6389768 | tf_op jit(solution)/shard_map/ppermute | solution.py:26
  46.0 8.8 %copy-start.4 = (s32[2,4,1,1]{1,3,2,0:T(1,128)S(1)}, s32[2,4,1,1]{1,3,2,0:T(1,128)}, u32[]{:S(2)}) copy-start(s32[2,4,1,1]{1,3,2,0:T(1,128)} %param.7) | copy-start | bytes 100
  46.0 60.2 %copy-start.2 = (f32[4,256,1024]{1,0,2:T(4,128)S(1)}, f32[4,256,1024]{1,0,2:T(4,128)}, u32[]{:S(2)}) copy-start(f32[4,256,1024]{1,0,2:T(4,128)} %copy.28) | copy-start | bytes 12582916
  49.5 56.7 %collective-permute-start.2 = (f32[4,516,130]{1,0,2:T(4,128)S(1)}, f32[4,516,130]{1,0,2:T(4,128)S(1)}, u32[]{:S(2)}, u32[]{:S(2)}) collective-permute-start(f32[4,516,130]{1,0,2:T(4,128)S(1)} %get-tuple-element.44), channel_id=1, source_target_pairs={{0,1},{1,2},{2,3},{3,4},{4,5},{5,6},{6,7},{8,9},{9,10},{10,11},{11... | collective-permute-start | bytes 3219848 | tf_op jit(solution)/shard_map/ppermute | solution.py:25
  52.8 53.3 %collective-permute-start.3 = (f32[4,516,130]{1,0,2:T(4,128)S(1)}, f32[4,516,130]{1,0,2:T(4,128)S(1)}, u32[]{:S(2)}, u32[]{:S(2)}) collective-permute-start(f32[4,516,130]{1,0,2:T(4,128)S(1)} %get-tuple-element.45), channel_id=1, source_target_pairs={{1,0},{2,1},{3,2},{4,3},{5,4},{6,5},{7,6},{9,8},{10,9},{11,10},{12... | collective-permute-start | bytes 3219848 | tf_op jit(solution)/shard_map/ppermute | solution.py:26
  172.2 9.2 %copy-start.3 = (f32[4,256,1024]{2,1,0:T(8,128)S(1)}, f32[4,256,1024]{2,1,0:T(8,128)}, u32[]{:S(2)}) copy-start(f32[4,256,1024]{2,1,0:T(8,128)} %param.4) | copy-start | bytes 12582916
  184.9 13.9 %copy-start = (f32[4,256,1024]{2,1,0:T(8,128)}, f32[4,256,1024]{2,1,0:T(8,128)S(1)}, u32[]{:S(2)}) copy-start(f32[4,256,1024]{2,1,0:T(8,128)S(1)} %fusion.25) | copy-start | bytes 12582916
  184.9 9.4 %collective-permute-start.4 = (f32[4,4,1024]{2,1,0:T(4,128)S(1)}, f32[4,4,1024]{2,1,0:T(4,128)S(1)}, u32[]{:S(2)}, u32[]{:S(2)}) collective-permute-start(f32[4,4,1024]{2,1,0:T(4,128)S(1)} %get-tuple-element.55), channel_id=1, source_target_pairs={{0,8},{8,16},{16,24},{24,32},{32,40},{40,48},{48,56},{56,64},{64,7... | collective-permute-start | bytes 196616 | tf_op jit(solution)/shard_map/ppermute | solution.py:25
  192.4 5.8 %collective-permute-start.5 = (f32[4,4,1024]{2,1,0:T(4,128)S(1)}, f32[4,4,1024]{2,1,0:T(4,128)S(1)}, u32[]{:S(2)}, u32[]{:S(2)}) collective-permute-start(f32[4,4,1024]{2,1,0:T(4,128)S(1)} %get-tuple-element.56), channel_id=1, source_target_pairs={{8,0},{16,8},{24,16},{32,24},{40,32},{48,40},{56,48},{64,56},{72,6... | collective-permute-start | bytes 196616 | tf_op jit(solution)/shard_map/ppermute | solution.py:26
  199.3 5.9 %collective-permute-start.6 = (f32[4,264,4]{1,2,0:T(4,128)S(1)}, f32[4,264,4]{1,2,0:T(4,128)S(1)}, u32[]{:S(2)}, u32[]{:S(2)}) collective-permute-start(f32[4,264,4]{1,2,0:T(4,128)S(1)} %copy.32), channel_id=1, source_target_pairs={{0,1},{1,2},{2,3},{3,4},{4,5},{5,6},{6,7},{8,9},{9,10},{10,11},{11... | collective-permute-start | bytes 50696 | tf_op jit(solution)/shard_map/ppermute | solution.py:25
  203.7 5.1 %collective-permute-start.7 = (f32[4,264,4]{1,2,0:T(4,128)S(1)}, f32[4,264,4]{1,2,0:T(4,128)S(1)}, u32[]{:S(2)}, u32[]{:S(2)}) collective-permute-start(f32[4,264,4]{1,2,0:T(4,128)S(1)} %copy.34), channel_id=1, source_target_pairs={{1,0},{2,1},{3,2},{4,3},{5,4},{6,5},{7,6},{9,8},{10,9},{11,10},{12... | collective-permute-start | bytes 50696 | tf_op jit(solution)/shard_map/ppermute | solution.py:26
  327.7 5.5 %collective-permute-start.8 = (f32[4,1,64]{2,1,0:T(1,128)S(1)}, f32[4,1,64]{2,1,0:T(1,128)S(1)}, u32[]{:S(2)}, u32[]{:S(2)}) collective-permute-start(f32[4,1,64]{2,1,0:T(1,128)S(1)} %get-tuple-element.61), channel_id=1, source_target_pairs={{0,8},{8,16},{16,24},{24,32},{32,40},{40,48},{48,56},{56,64},{64,7... | collective-permute-start | bytes 3080 | tf_op jit(solution)/shard_map/ppermute | solution.py:25
  331.2 4.9 %collective-permute-start.9 = (f32[4,1,64]{2,1,0:T(1,128)S(1)}, f32[4,1,64]{2,1,0:T(1,128)S(1)}, u32[]{:S(2)}, u32[]{:S(2)}) collective-permute-start(f32[4,1,64]{2,1,0:T(1,128)S(1)} %get-tuple-element.62), channel_id=1, source_target_pairs={{8,0},{16,8},{24,16},{32,24},{40,32},{48,40},{56,48},{64,56},{72,6... | collective-permute-start | bytes 3080 | tf_op jit(solution)/shard_map/ppermute | solution.py:26
  336.2 2.9 collective-permute-start.10
  337.5 4.8 %collective-permute-start.11 = (f32[4,18,1]{2,1,0:T(8,128)S(1)}, f32[4,18,1]{2,1,0:T(8,128)S(1)}, u32[]{:S(2)}, u32[]{:S(2)}) collective-permute-start(f32[4,18,1]{2,1,0:T(8,128)S(1)} %get-tuple-element.60), channel_id=1, source_target_pairs={{1,0},{2,1},{3,2},{4,3},{5,4},{6,5},{7,6},{9,8},{10,9},{11,10},{12... | collective-permute-start | bytes 872 | tf_op jit(solution)/shard_map/ppermute | solution.py:26
  348.9 8.2 %copy-start.1 = (f32[4,256,1024]{2,1,0:T(8,128)}, f32[4,256,1024]{2,1,0:T(8,128)S(1)}, u32[]{:S(2)}) copy-start(f32[4,256,1024]{2,1,0:T(8,128)S(1)} %convolution_subtract_fusion) | copy-start | bytes 12582916
  349.0 7.2 %collective-permute-start.12 = (f32[4,1,1024]{2,1,0:T(1,128)S(1)}, f32[4,1,1024]{2,1,0:T(1,128)S(1)}, u32[]{:S(2)}, u32[]{:S(2)}) collective-permute-start(f32[4,1,1024]{2,1,0:T(1,128)S(1)} %get-tuple-element.54), channel_id=1, source_target_pairs={{0,8},{8,16},{16,24},{24,32},{32,40},{40,48},{48,56},{56,64},{64,7... | collective-permute-start | bytes 49160 | tf_op jit(solution)/shard_map/ppermute | solution.py:25
  352.1 5.1 %collective-permute-start.13 = (f32[4,1,1024]{2,1,0:T(1,128)S(1)}, f32[4,1,1024]{2,1,0:T(1,128)S(1)}, u32[]{:S(2)}, u32[]{:S(2)}) collective-permute-start(f32[4,1,1024]{2,1,0:T(1,128)S(1)} %get-tuple-element.53), channel_id=1, source_target_pairs={{8,0},{16,8},{24,16},{32,24},{40,32},{48,40},{56,48},{64,56},{72,6... | collective-permute-start | bytes 49160 | tf_op jit(solution)/shard_map/ppermute | solution.py:26
  357.6 5.9 %collective-permute-start.14 = (f32[4,258,1]{1,0,2:T(4,128)S(1)}, f32[4,258,1]{1,0,2:T(4,128)S(1)}, u32[]{:S(2)}, u32[]{:S(2)}) collective-permute-start(f32[4,258,1]{1,0,2:T(4,128)S(1)} %copy.38), channel_id=1, source_target_pairs={{1,0},{2,1},{3,2},{4,3},{5,4},{6,5},{7,6},{9,8},{10,9},{11,10},{12... | collective-permute-start | bytes 12392 | tf_op jit(solution)/shard_map/ppermute | solution.py:26
  359.2 5.1 %collective-permute-start.15 = (f32[4,258,1]{1,0,2:T(4,128)S(1)}, f32[4,258,1]{1,0,2:T(4,128)S(1)}, u32[]{:S(2)}, u32[]{:S(2)}) collective-permute-start(f32[4,258,1]{1,0,2:T(4,128)S(1)} %copy.40), channel_id=1, source_target_pairs={{0,1},{1,2},{2,3},{3,4},{4,5},{5,6},{6,7},{8,9},{9,10},{10,11},{11... | collective-permute-start | bytes 12392 | tf_op jit(solution)/shard_map/ppermute | solution.py:25
